TPU v7x, 32 devices: a whole 2x2x4 slice. The times are simulated.
32 devices in a mesh: ang: 8 (over z, y), row: 4 (over x, core).
Axes of the slice: x: 2, y: 2, z: 4, core: 2. Of those that a mesh axis runs over, the one named last changes fastest.
Arguments:
- raw: bfloat16 [2304, 2048], P(('row', 'ang')), parts along dimension 0, may hold values from 6e-05 to 1, as said below
- block_dest: int32 [576], P('ang'), may hold values from 0 to 575, as said below
- section_offset: int32 [64, 9], P('ang'), may hold values from 0 to 14336, as said below
- ramp_length: int32 [9], replicated, may hold values from 16 to 256
- module_width: int32 [8], replicated, may hold values from 1 to 4096, 16384 in all
Outputs:
- filtered: float32 [256, 16384], P(('row', 'ang')), parts along dimension 0
There are 4 independent parts, one for each index of `row`. A program takes and returns all parts, laid end to end along the dimension named above; an argument that names none is the same for every part. Nothing has to cross between parts.
Inputs may be any that keep to these rules, and one draw needn't show every extreme that they name: `block_dest`: A permutation of the tile rows. Each index of ang holds 72 of them, at most 9 for any one index of ang that owns their angle (angle a is owned by index a // 8), and in every draw some index holds exactly 9 for some owner. `section_offset`: tile 0 starts at column 0 and the last tile at 14336 at every angle; tile t otherwise lies within 64 columns of t * 1792. `module_width`: the widths sum to 16384; the widest module has exactly 4096 columns. `raw`: positive intensities.
All inputs are finite; a program needn't handle non-finite values.
Results may differ from a plain program's by a relative error of at most 0.0014.
Values may be sent and summed in bfloat16 or wider, within the bound.
A program may use at most 64 MiB of HBM per device.

v0:
```python
import math

import jax
import jax.numpy as jnp
from jax import lax
from jax.sharding import PartitionSpec as P

W = 16384
RAMP_HALF = 128


SHRINK_SCALE = 1.0
EPSILON = 1e-06


def ramp_taps(offsets):
    values = offsets.astype(jnp.float32)
    nonzero = jnp.where(offsets == 0, jnp.float32(1.0), values)
    odd_mask = offsets % 2 != 0
    taps = jnp.where(odd_mask, -1.0 / (math.pi * math.pi * nonzero * nonzero), jnp.float32(0.0))
    taps = jnp.where(offsets == 0, jnp.float32(0.25), taps)
    return jnp.where(jnp.abs(offsets) <= RAMP_HALF, taps, jnp.float32(0.0))


def phase_table(rows_count, cols_count, modulus):
    product = (
        jnp.arange(rows_count, dtype=jnp.int32)[:, None]
        * jnp.arange(cols_count, dtype=jnp.int32)[None, :]
    )
    phase = 2.0 * math.pi / modulus * (product % modulus).astype(jnp.float32)
    return (jnp.cos(phase), -jnp.sin(phase))


def dft_tables(angles):
    first = min(64, angles)
    second = angles // first
    first_real, first_imag = phase_table(first, first, first)
    twid_real, twid_imag = phase_table(first, second, angles)
    second_real, second_imag = phase_table(second, second, second)
    freqs = (
        jnp.arange(first, dtype=jnp.int32)[:, None]
        + first * jnp.arange(second, dtype=jnp.int32)[None, :]
    )
    wrapped = jnp.minimum(freqs, angles - freqs).astype(jnp.float32)
    band_weight = jnp.exp(-wrapped / (angles // 8))
    return (first_real, first_imag, twid_real, twid_imag, second_real, second_imag, band_weight)


def einsum_high(form, left, right):
    return jnp.einsum(form, left, right, precision=lax.Precision.HIGHEST)


def forward_dft(signal, tables):
    first_real, first_imag, twid_real, twid_imag, second_real, second_imag, band_weight = tables
    first = first_real.shape[0]
    second = second_real.shape[0]
    shaped = signal.reshape(first, second, signal.shape[1])
    step_real = einsum_high("kn,nmc->kmc", first_real, shaped)
    step_imag = einsum_high("kn,nmc->kmc", first_imag, shaped)
    turned_real = step_real * twid_real[:, :, None] - step_imag * twid_imag[:, :, None]
    turned_imag = step_real * twid_imag[:, :, None] + step_imag * twid_real[:, :, None]
    out_real = einsum_high("qm,kmc->kqc", second_real, turned_real) - einsum_high(
        "qm,kmc->kqc", second_imag, turned_imag
    )
    out_imag = einsum_high("qm,kmc->kqc", second_real, turned_imag) + einsum_high(
        "qm,kmc->kqc", second_imag, turned_real
    )
    return (out_real, out_imag)


def inverse_dft(spec_real, spec_imag, tables):
    first_real, first_imag, twid_real, twid_imag, second_real, second_imag, band_weight = tables
    first = first_real.shape[0]
    second = second_real.shape[0]
    back_real = einsum_high("qm,kqc->kmc", second_real, spec_real) + einsum_high(
        "qm,kqc->kmc", second_imag, spec_imag
    )
    back_imag = einsum_high("qm,kqc->kmc", second_real, spec_imag) - einsum_high(
        "qm,kqc->kmc", second_imag, spec_real
    )
    turned_real = back_real * twid_real[:, :, None] + back_imag * twid_imag[:, :, None]
    turned_imag = back_imag * twid_real[:, :, None] - back_real * twid_imag[:, :, None]
    signal = einsum_high("kn,kmc->nmc", first_real, turned_real) + einsum_high(
        "kn,kmc->nmc", first_imag, turned_imag
    )
    return signal.reshape(first * second, spec_real.shape[2]) / (first * second)


def remove_stripes(spec_real, spec_imag, magnitude, level_col, tables):
    band_weight = tables[6]
    factor = jnp.maximum(magnitude - level_col[None, None, :], 0.0) / jnp.maximum(
        magnitude, level_col[None, None, :]
    )
    factor = factor * band_weight[:, :, None]
    return inverse_dft(spec_real * factor, spec_imag * factor, tables)


def add_window(target, piece, start):
    zero = jnp.int32(0)
    current = lax.dynamic_slice(target, (zero, start), piece.shape)
    return lax.dynamic_update_slice(target, current + piece, (zero, start))


def per_device(raw, block_dest, section_offset, ramp_length, module_width):
    devices = lax.axis_size("ang")
    my_index = lax.axis_index("ang")
    blocks_here = raw.shape[0]
    tile_width = raw.shape[1]
    angles_here = section_offset.shape[0]
    tiles = section_offset.shape[1]
    angles = angles_here * devices
    capacity = (blocks_here + devices - 1) // devices
    modules = module_width.shape[0]
    widest = 2 * W // devices
    owners = block_dest // blocks_here
    owner_hot = (owners[:, None] == jnp.arange(devices, dtype=jnp.int32)[None, :]).astype(jnp.int32)
    slot_rank = jnp.sum((jnp.cumsum(owner_hot, axis=0) - owner_hot) * owner_hot, axis=1)
    slot = owners * capacity + slot_rank
    send_match = jnp.arange(devices * capacity, dtype=jnp.int32)[:, None] == slot[None, :]
    outgoing = jnp.dot(
        send_match.astype(raw.dtype), raw, preferred_element_type=jnp.float32
    ).astype(raw.dtype)
    out_ids = jnp.sum(jnp.where(send_match, block_dest[None, :] + 1, 0), axis=1) - 1
    arrived, arrived_ids = (
        lax.all_to_all(
            outgoing.reshape(devices, capacity, tile_width),
            "ang",
            split_axis=0,
            concat_axis=0,
            tiled=True,
        ),
        lax.all_to_all(
            out_ids.reshape(devices, capacity), "ang", split_axis=0, concat_axis=0, tiled=True
        ),
    )
    arrived = arrived.reshape(devices * capacity, tile_width)
    arrived_ids = arrived_ids.reshape(devices * capacity)
    local_slot = jnp.where(arrived_ids >= 0, arrived_ids - my_index * blocks_here, blocks_here)
    recv_match = (jnp.arange(blocks_here, dtype=jnp.int32)[:, None] == local_slot[None, :]).astype(
        arrived.dtype
    )
    tile_grid = jnp.dot(recv_match, arrived, preferred_element_type=jnp.float32)
    tile_grid = tile_grid.reshape(angles_here, tiles, tile_width)
    inner_cols = jnp.arange(tile_width, dtype=jnp.int32)
    edge = (jnp.minimum(inner_cols, tile_width - 1 - inner_cols) + 1).astype(jnp.float32)
    feather_tile = jnp.minimum(
        jnp.float32(1.0), edge[None, :] / ramp_length[:, None].astype(jnp.float32)
    )

    def blend_angle(angle, sums):
        weighted_sum, weight_sum = sums
        angle_tiles = lax.dynamic_index_in_dim(tile_grid, angle, 0, keepdims=False)
        offsets_here = lax.dynamic_index_in_dim(section_offset, angle, 0, keepdims=False)
        for tile in range(tiles):
            start = offsets_here[tile]
            weights = feather_tile[tile]
            place = (angle, start)
            current = lax.dynamic_slice(weighted_sum, place, (1, tile_width))
            weighted_sum = lax.dynamic_update_slice(
                weighted_sum, current + (weights * angle_tiles[tile])[None, :], place
            )
            current_w = lax.dynamic_slice(weight_sum, place, (1, tile_width))
            weight_sum = lax.dynamic_update_slice(weight_sum, current_w + weights[None, :], place)
        return (weighted_sum, weight_sum)

    zeros_rows = jnp.zeros((angles_here, W), jnp.float32)
    weighted_sum, weight_sum = lax.fori_loop(0, angles_here, blend_angle, (zeros_rows, zeros_rows))
    projection = -jnp.log(weighted_sum / weight_sum)
    bounds = jnp.cumsum(module_width)
    starts = bounds - module_width
    widths = module_width.astype(jnp.float32)
    window = jnp.arange(widest, dtype=jnp.int32)
    proj_pad = jnp.pad(projection, ((0, 0), (0, widest)))

    def center_module(module, acc):
        start = starts[module]
        piece = lax.dynamic_slice(proj_pad, (jnp.int32(0), start), (angles_here, widest))
        valid = (window < module_width[module])[None, :]
        mean = jnp.sum(jnp.where(valid, piece, 0.0), axis=1) / widths[module]
        update = jnp.where(valid, piece - mean[:, None], jnp.float32(0.0))
        return add_window(acc, update, start)

    cent_pad = lax.fori_loop(
        0, modules, center_module, jnp.zeros((angles_here, W + widest), jnp.float32)
    )
    tables = dft_tables(angles)

    def cut_module(module, buffer):
        start = starts[module]
        piece = lax.dynamic_slice(cent_pad, (jnp.int32(0), start), (angles_here, widest))
        piece = jnp.where((window < module_width[module])[None, :], piece, jnp.float32(0.0))
        return lax.dynamic_update_slice(buffer, piece[None], (module, jnp.int32(0), jnp.int32(0)))

    outbound = lax.fori_loop(
        0, modules, cut_module, jnp.zeros((devices, angles_here, widest), jnp.float32)
    )
    mine = (
        lax.all_to_all(
            outbound.astype(jnp.bfloat16), "ang", split_axis=0, concat_axis=0, tiled=True
        )
        .astype(outbound.dtype)
        .reshape(angles, widest)
    )
    spec_real, spec_imag = forward_dft(mine, tables)
    magnitude = jnp.sqrt(spec_real * spec_real + spec_imag * spec_imag)
    my_valid = (window < module_width[my_index]).astype(jnp.float32)
    my_total = jnp.sum(jnp.sum(magnitude, axis=(0, 1)) * my_valid)
    level = SHRINK_SCALE * (my_total / (angles * widths[my_index]) + EPSILON)
    level_col = jnp.full((widest,), 1.0, jnp.float32) * level
    stripe = remove_stripes(spec_real, spec_imag, magnitude, level_col, tables) * my_valid[None, :]
    returned = lax.all_to_all(
        stripe.reshape(angles, 1, widest), "ang", split_axis=0, concat_axis=1, tiled=True
    )

    def put_module(module, acc):
        piece = lax.dynamic_index_in_dim(returned, module, 1, keepdims=False)
        return add_window(acc, piece, starts[module])

    stripe_pad = lax.fori_loop(
        0, modules, put_module, jnp.zeros((angles_here, W + widest), jnp.float32)
    )
    stripe_rows = stripe_pad[:, :W]
    clean = projection - stripe_rows
    block_count = W // RAMP_HALF
    blocked = clean.reshape(angles_here, block_count, RAMP_HALF)
    padded = jnp.pad(blocked, ((0, 0), (1, 1), (0, 0)))
    inner = jnp.arange(RAMP_HALF, dtype=jnp.int32)
    filtered = jnp.zeros((angles_here, block_count, RAMP_HALF), jnp.float32)
    for shift_block in (-1, 0, 1):
        lag = inner[None, :] - inner[:, None] - RAMP_HALF * shift_block
        matrix = ramp_taps(lag)
        source = padded[:, 1 + shift_block : 1 + shift_block + block_count, :]
        filtered = filtered + einsum_high("abi,io->abo", source, matrix)
    return filtered.reshape(angles_here, W)


def solution(mesh):
    in_specs = (P(("row", "ang"), None), P("ang"), P("ang", None), P(), P())
    out_specs = P(("row", "ang"), None)
    return jax.shard_map(
        per_device, mesh=mesh, in_specs=in_specs, out_specs=out_specs, check_vma=False
    )
```

profile of v0, /device:TPU:0, one launch (start us, length us, event | category | flops | bytes accessed | tf_op | source)
XLA Modules:
  0.0 484.8 jit_solution(15067246593910627022)
XLA Ops:
  1.9 7.3 %all-to-all-start = ((s32[8,1,9]{2,1,0:T(1,128)}), s32[8,1,9]{2,1,0:T(1,128)S(1)}, u32[]{:S(2)}, u32[]{:S(2)}) async-start(s32[8,1,9]{2,1,0:T(1,128)} %bitcast.20), calls=%async_computation | async-start | bytes 8192 | tf_op jit(solution)/shard_map/all_to_all | solution.py:132
  11.3 4.4 all-to-all-done
  15.7 3.5 all-to-all-start.1
  19.4 13.1 %all-to-all-done.1 = bf16[8,9,2048]{2,1,0:T(8,128)(2,1)S(1)} async-done(((bf16[8,9,2048]{2,1,0:T(8,128)(2,1)}), bf16[8,9,2048]{2,1,0:T(8,128)(2,1)S(1)}, u32[]{:S(2)}, u32[]{:S(2)}) %all-to-all-start.1) | async-done | bytes 294944 | tf_op jit(solution)/shard_map/all_to_all | solution.py:125
  33.0 267.6 %while.56 = (s32[]{:T(128)}, f32[8,16384]{1,0:T(8,128)S(1)}, f32[8,16384]{1,0:T(8,128)S(1)}, s32[8,9]{1,0:T(8,128)}, f32[9,2048]{1,0:T(8,128)S(1)}, /*index=5*/f...) while((s32[]{:T(128)}, f32[8,16384]{1,0:T(8,128)S(1)}, ...), condition=%wide.region_4.5_spmd, body=%wide.region_3.4_spmd.sunk | while | flops 55333 | bytes 811931 | solution.py:167
  300.9 53.5 %while.58 = (s32[]{:T(128)}, f32[8,20480]{1,0:T(8,128)S(1)}, s32[8]{0:T(128)S(1)}, s32[8]{0:T(128)S(1)}, f32[8,20480]{1,0:T(8,128)S(1)}, /*index=5*/f32[8]{0:T(128)S(1)}, s32[]{:T(128)}, s32[]{:T(128)}, s32[]{:T(128)}) while((s32[]{:T(128)}, f32[8,20480]{1,0:T(8,128)S(1)}, s32[8]{0:T(128)S(1)}, s32[8]{0:T(128)S(1)}, ...), condition=%wide.region_8.9_spmd.clone, body=%wide.region_6.8_spmd.clone.sunk | while | flops 167941 | bytes 799031 | solution.py:183
  306.3 1.1 dynamic_update_slice.190
  312.8 1.3 dynamic_update_slice.190
  319.5 1.3 dynamic_update_slice.190
  326.3 1.3 dynamic_update_slice.190
  333.0 1.3 dynamic_update_slice.190
  339.7 1.3 dynamic_update_slice.190
  346.4 1.3 dynamic_update_slice.190
  353.2 1.2 dynamic_update_slice.190
  354.5 36.0 %while.59 = (s32[]{:T(128)}, bf16[8,8,4096]{2,1,0:T(8,128)(2,1)}, s32[8]{0:T(128)S(1)}, s32[8]{0:T(128)S(1)}, bf16[8,20480]{1,0:T(8,128)(2,1)S(1)}, /*index=5*/s32[]{:T(128)}, s32[]{:T(128)}, s32[]{:T(128)}) while((s32[]{:T(128)}, bf16[8,8,4096]{2,1,0:T(8,128)(2,1)}, s32[8]{0:T(128)S(1)}, s32[8]{0:T(128)S(1)}, ...), condition=%wide.region_10.11_spmd.clone, body=%wide.region_9.10_spmd.clone.sunk | while | flops 36869 | bytes 139927 | solution.py:194
  390.4 3.7 all-to-all-start.2
  396.7 11.3 %all-to-all-done.2 = bf16[8,8,4096]{2,1,0:T(8,128)(2,1)S(1)} async-done(((bf16[8,8,4096]{2,1,0:T(8,128)(2,1)}), bf16[8,8,4096]{2,1,0:T(8,128)(2,1)S(1)}, u32[]{:S(2)}, u32[]{:S(2)}) %all-to-all-start.2) | async-done | bytes 524320 | tf_op jit(solution)/shard_map/all_to_all | solution.py:198
  408.7 2.3 fusion.37
  411.0 1.3 select_reduce_fusion.3
  413.0 3.5 fusion.27
  416.5 2.2 fusion.23
  418.8 2.0 copy.10
  420.8 3.7 all-to-all-start.3
  424.5 25.6 %all-to-all-done.3 = f32[64,1,4096]{2,1,0:T(1,128)S(1)} async-done(((f32[64,1,4096]{2,1,0:T(1,128)}), f32[64,1,4096]{2,1,0:T(1,128)S(1)}, u32[]{:S(2)}, u32[]{:S(2)}) %all-to-all-start.3) | async-done | bytes 1048608 | tf_op jit(solution)/shard_map/all_to_all | solution.py:211
  450.7 31.0 %while.57 = (s32[]{:T(128)}, f32[8,20480]{1,0:T(8,128)S(1)}, s32[8]{0:T(128)S(1)}, f32[8,8,4096]{2,0,1:T(8,128)S(1)}, s32[]{:T(128)}, /*index=5*/s32[]{:T(128)}, s32[]{:T(128)}) while((s32[]{:T(128)}, f32[8,20480]{1,0:T(8,128)S(1)}, s32[8]{0:T(128)S(1)}, f32[8,8,4096]{2,0,1:T(8,128)S(1)}, s32[]{:T(128)}, /*index=5*/s32[]{:T(128)}, ...), condition=%wide.region_14.15_spmd, body=%wide.region_13.14_spmd.sunk | while | flops 32773 | bytes 655495 | solution.py:219
  457.0 1.3 dynamic_update_slice.189
  460.9 1.3 dynamic_update_slice.189
  464.8 1.3 dynamic_update_slice.189
  468.7 1.3 dynamic_update_slice.189
  472.6 1.3 dynamic_update_slice.189
  476.5 1.3 dynamic_update_slice.189
  480.4 1.2 dynamic_update_slice.189
  (393 shorter events, 195.1 us)
Async XLA Ops:
  0.0 9.2 %copy-start = (bf16[72,2048]{1,0:T(8,128)(2,1)S(1)}, bf16[72,2048]{1,0:T(8,128)(2,1)}, u32[]{:S(2)}) copy-start(bf16[72,2048]{1,0:T(8,128)(2,1)} %param.13) | copy-start | bytes 884740
  1.9 13.8 %all-to-all-start = ((s32[8,1,9]{2,1,0:T(1,128)}), s32[8,1,9]{2,1,0:T(1,128)S(1)}, u32[]{:S(2)}, u32[]{:S(2)}) async-start(s32[8,1,9]{2,1,0:T(1,128)} %bitcast.20), calls=%async_computation | async-start | bytes 8192 | tf_op jit(solution)/shard_map/all_to_all | solution.py:132
  9.5 0.7 copy-start.1
  10.3 0.9 copy-start.2
  15.7 16.8 %all-to-all-start.1 = ((bf16[8,9,2048]{2,1,0:T(8,128)(2,1)}), bf16[8,9,2048]{2,1,0:T(8,128)(2,1)S(1)}, u32[]{:S(2)}, u32[]{:S(2)}) async-start(bf16[8,9,2048]{2,1,0:T(8,128)(2,1)} %reshape.313), calls=%async_computation.1 | async-start | bytes 1048576 | tf_op jit(solution)/shard_map/all_to_all | solution.py:125
  390.4 17.5 %all-to-all-start.2 = ((bf16[8,8,4096]{2,1,0:T(8,128)(2,1)}), bf16[8,8,4096]{2,1,0:T(8,128)(2,1)S(1)}, u32[]{:S(2)}, u32[]{:S(2)}) async-start(bf16[8,8,4096]{2,1,0:T(8,128)(2,1)} %get-tuple-element.430), calls=%async_computation.2 | async-start | bytes 1048576 | tf_op jit(solution)/shard_map/all_to_all | solution.py:198
  413.0 3.5 copy-start.3
  420.8 29.2 %all-to-all-start.3 = ((f32[64,1,4096]{2,1,0:T(1,128)}), f32[64,1,4096]{2,1,0:T(1,128)S(1)}, u32[]{:S(2)}, u32[]{:S(2)}) async-start(f32[64,1,4096]{2,1,0:T(1,128)} %copy.10), calls=%async_computation.3 | async-start | bytes 2097152 | tf_op jit(solution)/shard_map/all_to_all | solution.py:211
where the time goes:
time: 488 us; the launch traced here: 485 us
  loops' own time  185 us (38%)
  local copies, waits for them, and re-layouts  177 us (36%)
  waiting for transfers between devices  54.4 us (11%)
  other arithmetic  37.8 us (8%)
  starting transfers between devices  18.2 us (4%)
  matrix products  11.1 us (2%)
    another operation x1, loops' own time, per_device(): lax.fori_loop(0, angles_here, blend_angle, (zeros_rows, zeros_rows))  138 us
    dynamic_update_slice x72, local copies, waits for them, and re-layouts, blend_angle(): lax.dynamic_update_slice(weight_sum, current_w + weights[None, :], place)  54.8 us
    dynamic_update_slice x72, local copies, waits for them, and re-layouts, blend_angle(): lax.dynamic_update_slice(weighted_sum, current + (weights * angle_tiles[t...  54.8 us
    all_to_all x1, waiting for transfers between devices, per_device(): lax.all_to_all(stripe.reshape(angles, 1, widest), 'ang', split_axis=0, co...  25.6 us
    dynamic_update_slice x16, local copies, waits for them, and re-layouts, add_window(): return lax.dynamic_update_slice(target, current + piece, (zero, start))  20.4 us
    another operation x1, loops' own time, per_device(): lax.fori_loop(0, modules, center_module, jnp.zeros((angles_here, W + wide...  15.9 us
    another operation x1, loops' own time, per_device(): lax.fori_loop(0, modules, cut_module, jnp.zeros((devices, angles_here, wi...  15.6 us
    another operation x1, loops' own time, per_device(): lax.fori_loop(0, modules, put_module, jnp.zeros((angles_here, W + widest)...  15.1 us
  transfers between devices with their start and end apart: 4, of which 4 were waited for; matrix products, arithmetic and copies ran while one was open for 1% of the time, Pallas kernels for 0%

commit v1 on v0

v1 whole, which is shorter than its diff:
```python
import functools
import math

import jax
import jax.numpy as jnp
import ml_dtypes
import numpy as np
from jax import lax
from jax.experimental import pallas as pl
from jax.experimental.pallas import tpu as pltpu
from jax.sharding import PartitionSpec as P

W = 16384
RAMP_HALF = 128
JITTER = 64
SHRINK_SCALE = 1.0
EPSILON = 1e-06
LANES = 128
SPAN = 2048

F32 = jnp.float32
BF16 = jnp.bfloat16


def split_np(table):
    high = table.astype(ml_dtypes.bfloat16)
    low = (table - high.astype(np.float64)).astype(ml_dtypes.bfloat16)
    return high, low


def freq_rows(angles):
    return -(-(angles // 2 + 1) // 8) * 8


def forward_table(angles, devices, fold):
    rows = freq_rows(angles)
    here = angles // devices
    k = np.arange(rows)[:, None]
    a = np.arange(angles)[None, :]
    phase = 2.0 * np.pi * ((k * a) % angles) / angles
    keep = (k <= angles // 2).astype(np.float64)
    table = np.concatenate([np.cos(phase) * keep, -np.sin(phase) * keep], axis=0)
    placed = np.zeros((fold, 2 * rows, devices, fold, here))
    for part in range(fold):
        placed[part, :, :, part, :] = table.reshape(2 * rows, devices, here)
    high, low = split_np(placed.reshape(fold, 2 * rows, devices * fold * here))
    return np.concatenate([high, low], axis=1)


def inverse_table(angles):
    rows = freq_rows(angles)
    k = np.arange(rows)[None, :]
    a = np.arange(angles)[:, None]
    phase = 2.0 * np.pi * ((k * a) % angles) / angles
    twice = np.where((k == 0) | (2 * k == angles), 1.0, 2.0) * (k <= angles // 2)
    weight = twice * np.exp(-np.minimum(k, angles - k) / (angles // 8)) / angles
    table = np.concatenate([np.cos(phase) * weight, -np.sin(phase) * weight], axis=1)
    high, low = split_np(table)
    return np.concatenate([high, high, low], axis=1)


def ramp_table():
    i = np.arange(3 * LANES)[:, None] - LANES
    n = np.arange(LANES)[None, :] - i
    safe = np.where(n == 0, 1, n).astype(np.float64)
    taps = np.where(n % 2 != 0, -1.0 / (np.pi * np.pi * safe * safe), 0.0)
    taps = np.where(n == 0, 0.25, taps)
    taps = np.where(np.abs(n) <= RAMP_HALF, taps, 0.0)
    high, low = split_np(taps)
    return np.stack([high, low])


def dot(left, right):
    return jnp.dot(left, right, preferred_element_type=F32)


def dot_nt(left, right):
    return lax.dot_general(left, right, (((1,), (1,)), ((), ())), preferred_element_type=F32)


def halves(x):
    high = x.astype(BF16)
    return high, (x - high.astype(F32)).astype(BF16)


def thirds(x):
    high = x.astype(BF16).astype(F32)
    rest = x - high
    mid = rest.astype(BF16).astype(F32)
    low = rest - mid
    return jnp.concatenate([high, mid, low, jnp.zeros_like(x)], axis=0).astype(BF16)


def iota(shape, axis):
    return lax.broadcasted_iota(jnp.int32, shape, axis)


def loop(count, body):
    if count <= 8:
        for step in range(count):
            body(step)
    else:

        def run(step, carry):
            body(step)
            return carry

        lax.fori_loop(0, count, run, 0)


def kernel(
    cfg,
    arrived_ref,
    offset_ref,
    ramp_ref,
    width_ref,
    fwd_ref,
    inv_ref,
    taps_ref,
    out_ref,
    grid_ref,
    sum_ref,
    weight_ref,
    proj_ref,
    cent_send,
    cent_recv,
    spec_ref,
    level_send,
    level_recv,
    stripe_send,
    stripe_recv,
    send_sem,
    recv_sem,
):
    devices, angles_here, tiles, tile_width, mods, fold = cfg
    angles = devices * angles_here
    cols = W // devices
    half = cols // fold
    rows = freq_rows(angles)
    step_cols = (W - tile_width) // (tiles - 1)
    window = tile_width + 2 * LANES
    blocks = angles_here * tiles
    me = lax.axis_index("ang")

    def peer_at(hop):
        return lax.rem(me + hop, devices)

    barrier = pltpu.get_barrier_semaphore()

    def greet(step):
        pl.semaphore_signal(
            barrier,
            inc=1,
            device_id={"ang": peer_at(step + 1)},
            device_id_type=pl.DeviceIdType.MESH,
        )

    loop(devices - 1, greet)

    def remote(phase, src, dst, slot, peer):
        return pltpu.make_async_remote_copy(
            src_ref=src,
            dst_ref=dst,
            send_sem=send_sem.at[phase, peer],
            recv_sem=recv_sem.at[phase, slot],
            device_id={"ang": peer},
            device_id_type=pl.DeviceIdType.MESH,
        )

    pick = (iota((8, LANES), 1) == 0).astype(F32).astype(BF16)
    ids = dot_nt(pick, arrived_ref[:, tile_width:])[0:1, :]
    row = iota((blocks, 1), 0).astype(F32)
    tile_of = jnp.floor((row + 0.5) * (1.0 / angles_here))
    wanted = (row - tile_of * angles_here) * tiles + tile_of + 1.0
    match = jnp.where(wanted == ids, 1.0, 0.0).astype(BF16)
    grid_ref[...] = dot(match, arrived_ref[:, :tile_width])

    sum_ref[...] = jnp.zeros_like(sum_ref)
    weight_ref[...] = jnp.zeros_like(weight_ref)
    inverse_ramp = 1.0 / ramp_ref[...].astype(F32)
    lane = iota((angles_here, window), 1)
    for tile in range(tiles):
        base = tile * step_cols
        shift = jnp.broadcast_to(
            offset_ref[:, tile : tile + 1] - (base - LANES), (angles_here, window)
        )
        piece = jnp.concatenate(
            [
                grid_ref[tile * angles_here : (tile + 1) * angles_here, :],
                jnp.zeros((angles_here, 2 * LANES), F32),
            ],
            axis=1,
        )
        for bit in range(8):
            moved = pltpu.roll(piece, 1 << bit, 1)
            piece = jnp.where((shift & (1 << bit)) != 0, moved, piece)
        x = lane - shift
        edge = (jnp.minimum(x, tile_width - 1 - x) + 1).astype(F32)
        feather = jnp.minimum(1.0, edge * inverse_ramp[:, tile : tile + 1])
        feather = jnp.maximum(feather, 0.0)
        sum_ref[:, base : base + window] += feather * piece
        weight_ref[:, base : base + window] += feather

    wide = width_ref[...]
    upper = iota((mods, mods), 1)
    lower = iota((mods, mods), 0)
    bounds = jnp.sum(jnp.where(upper <= lower, wide, 0.0), axis=1, keepdims=True)
    starts = jnp.sum(jnp.where(upper < lower, wide, 0.0), axis=1, keepdims=True)
    safe_wide = jnp.maximum(wide, 1.0)

    def member(first, count):
        c = (iota((mods, count), 1) + first).astype(F32)
        inside = (c >= starts) & (c < bounds)
        return jnp.where(inside, 1.0, 0.0).astype(BF16)

    def project(step, total):
        at = pl.multiple_of(step * SPAN, LANES)
        behind = pl.multiple_of(step * SPAN + LANES, LANES)
        blended = sum_ref[:, pl.ds(behind, SPAN)] / weight_ref[:, pl.ds(behind, SPAN)]
        projection = -jnp.log(blended)
        proj_ref[:, pl.ds(at, SPAN)] = projection
        return total + dot_nt(thirds(projection), member(at, SPAN))

    total = lax.fori_loop(0, W // SPAN, project, jnp.zeros((4 * angles_here, mods), F32))

    def gather_thirds(stack):
        a = angles_here
        return stack[0:a] + stack[a : 2 * a] + stack[2 * a : 3 * a]

    mean = thirds(gather_thirds(total) / safe_wide)

    pl.semaphore_wait(barrier, devices - 1)

    def centered_slab(owner):
        at = pl.multiple_of(owner * cols, LANES)
        flat = proj_ref[:, pl.ds(at, cols)] - gather_thirds(dot(mean, member(at, cols)))
        if fold > 1:
            flat = jnp.concatenate([flat[:, i * half : (i + 1) * half] for i in range(fold)], axis=0)
        return flat.astype(cent_send.dtype)

    def send_centered(step):
        peer = peer_at(step + 1)
        cent_send[peer] = centered_slab(peer)
        remote(0, cent_send.at[peer], cent_recv.at[me], me, peer).start()

    loop(devices - 1, send_centered)
    cent_recv[me] = centered_slab(me)

    def finish(phase, send_of, recv_of):
        def body(step):
            peer = peer_at(step + 1)
            copy = remote(phase, send_of(peer), recv_of(peer), peer, peer)
            copy.wait_recv()
            copy.wait_send()

        loop(devices - 1, body)

    finish(0, lambda p: cent_send.at[p], lambda p: cent_recv.at[p])

    signal = cent_recv[...].reshape(devices * fold * angles_here, half).astype(BF16)
    k = iota((rows, 1), 0)
    count_of = jnp.where((k == 0) | (2 * k == angles), 1.0, 2.0)
    count_of = jnp.where(2 * k <= angles, count_of, 0.0)
    mine = pl.multiple_of(me * cols, LANES)
    sums = jnp.zeros((4 * 8, mods), F32)
    for part in range(fold):
        wide_spec = dot(fwd_ref[part], signal)
        spectrum = wide_spec[: 2 * rows] + wide_spec[2 * rows :]
        spec_ref[part] = spectrum
        magnitude = jnp.sqrt(
            spectrum[:rows] * spectrum[:rows] + spectrum[rows:] * spectrum[rows:]
        )
        over_k = jnp.sum(magnitude * count_of, axis=0, keepdims=True)
        first_row = jnp.where(iota((8, half), 0) == 0, over_k, 0.0)
        sums = sums + dot_nt(thirds(first_row), member(mine + part * half, half))
    level_send[...] = jnp.zeros_like(level_send)
    level_send[:, 0:mods] = sums[0:8] + sums[8:16] + sums[16:24]

    def send_level(step):
        peer = peer_at(step + 1)
        remote(1, level_send, level_recv.at[me], me, peer).start()

    loop(devices - 1, send_level)
    level_recv[me] = level_send[...]
    finish(1, lambda p: level_send, lambda p: level_recv.at[p])
    everything = jnp.sum(level_recv[...], axis=0)[:, 0:mods]
    level = SHRINK_SCALE * (everything / (angles * safe_wide) + EPSILON)
    level_parts = thirds(jnp.where(iota((8, mods), 0) == 0, level, 0.0))

    for part in range(fold):
        spread = dot(level_parts, member(mine + part * half, half))
        level_col = spread[0:1] + spread[8:9] + spread[16:17]
        spectrum = spec_ref[part]
        magnitude = jnp.sqrt(
            spectrum[:rows] * spectrum[:rows] + spectrum[rows:] * spectrum[rows:]
        )
        factor = jnp.maximum(magnitude - level_col, 0.0) / jnp.maximum(magnitude, level_col)
        shrunk = jnp.concatenate([spectrum[:rows] * factor, spectrum[rows:] * factor], axis=0)
        high, low = halves(shrunk)
        stripe = dot(inv_ref[...], jnp.concatenate([high, low, high], axis=0))
        stripe_send[:, :, part * half : (part + 1) * half] = stripe.reshape(
            devices, angles_here, half
        )

    def send_stripe(step):
        peer = peer_at(step + 1)
        remote(2, stripe_send.at[peer], stripe_recv.at[me], me, peer).start()

    loop(devices - 1, send_stripe)
    stripe_recv[me] = stripe_send[me]
    finish(2, lambda p: stripe_send.at[p], lambda p: stripe_recv.at[p])

    sum_ref[:, 0:LANES] = jnp.zeros((angles_here, LANES), F32)
    sum_ref[:, W + LANES :] = jnp.zeros((angles_here, LANES), F32)

    def clean(owner):
        at = pl.multiple_of(owner * cols, LANES)
        behind = pl.multiple_of(owner * cols + LANES, LANES)
        sum_ref[:, pl.ds(behind, cols)] = proj_ref[:, pl.ds(at, cols)] - stripe_recv[owner]

    loop(devices, clean)
    lane_blocks = SPAN // LANES

    def ramp(step, carry):
        at = pl.multiple_of(step * SPAN, LANES)
        flat = sum_ref[:, pl.ds(at, SPAN + 2 * LANES)]
        stack = jnp.concatenate(
            [flat[:, b * LANES : (b + 1) * LANES] for b in range(lane_blocks + 2)], axis=0
        )
        n = lane_blocks * angles_here
        near = jnp.concatenate(
            [stack[s * angles_here : s * angles_here + n] for s in range(3)], axis=1
        )
        high, low = halves(near)
        done = dot(high, taps_ref[0]) + dot(low, taps_ref[0]) + dot(high, taps_ref[1])
        out_ref[:, pl.ds(at, SPAN)] = jnp.concatenate(
            [done[b * angles_here : (b + 1) * angles_here] for b in range(lane_blocks)], axis=1
        )
        return carry

    lax.fori_loop(0, W // SPAN, ramp, 0)


def per_device(raw, block_dest, section_offset, ramp_length, module_width):
    devices = lax.axis_size("ang")
    blocks_here = raw.shape[0]
    tile_width = raw.shape[1]
    angles_here, tiles = section_offset.shape
    angles = angles_here * devices
    capacity = (blocks_here + devices - 1) // devices
    owners = block_dest // blocks_here
    owner_hot = (owners[:, None] == jnp.arange(devices, dtype=jnp.int32)[None, :]).astype(jnp.int32)
    slot_rank = jnp.sum((jnp.cumsum(owner_hot, axis=0) - owner_hot) * owner_hot, axis=1)
    slot = owners * capacity + slot_rank
    send_match = jnp.arange(devices * capacity, dtype=jnp.int32)[:, None] == slot[None, :]
    local_id = (block_dest - owners * blocks_here + 1).astype(raw.dtype)
    extended = jnp.concatenate(
        [raw, jnp.broadcast_to(local_id[:, None], (blocks_here, LANES))], axis=1
    )
    outgoing = jnp.dot(
        send_match.astype(raw.dtype), extended, preferred_element_type=jnp.float32
    ).astype(raw.dtype)
    arrived = lax.all_to_all(
        outgoing.reshape(devices, capacity, tile_width + LANES),
        "ang",
        split_axis=0,
        concat_axis=0,
        tiled=True,
    ).reshape(devices * capacity, tile_width + LANES)

    cols = W // devices
    fold = 2 if cols % (2 * LANES) == 0 else 1
    wire = BF16 if fold == 2 else F32
    mods = -(-module_width.shape[0] // 16) * 16
    widths = jnp.pad(module_width, (0, mods - module_width.shape[0])).astype(F32)[None, :]
    half = cols // fold
    rows = freq_rows(angles)
    cfg = (devices, angles_here, tiles, tile_width, mods, fold)
    vmem = pl.BlockSpec(memory_space=pltpu.VMEM)
    return pl.pallas_call(
        functools.partial(kernel, cfg),
        out_shape=jax.ShapeDtypeStruct((angles_here, W), F32),
        in_specs=[vmem] * 7,
        out_specs=vmem,
        scratch_shapes=[
            pltpu.VMEM((angles_here * tiles, tile_width), F32),
            pltpu.VMEM((angles_here, W + 2 * LANES), F32),
            pltpu.VMEM((angles_here, W + 2 * LANES), F32),
            pltpu.VMEM((angles_here, W), F32),
            pltpu.VMEM((devices, angles_here * fold, half), wire),
            pltpu.VMEM((devices, angles_here * fold, half), wire),
            pltpu.VMEM((fold, 2 * rows, half), F32),
            pltpu.VMEM((8, max(mods, LANES)), F32),
            pltpu.VMEM((devices, 8, max(mods, LANES)), F32),
            pltpu.VMEM((devices, angles_here, cols), F32),
            pltpu.VMEM((devices, angles_here, cols), F32),
            pltpu.SemaphoreType.DMA((3, devices)),
            pltpu.SemaphoreType.DMA((3, devices)),
        ],
        compiler_params=pltpu.CompilerParams(
            collective_id=0, has_side_effects=True, vmem_limit_bytes=60 << 20
        ),
    )(
        arrived,
        section_offset,
        ramp_length[None, :],
        widths,
        jnp.asarray(forward_table(angles, devices, fold)),
        jnp.asarray(inverse_table(angles)),
        jnp.asarray(ramp_table()),
    )


def solution(mesh):
    in_specs = (P(("row", "ang"), None), P("ang"), P("ang", None), P(), P())
    out_specs = P(("row", "ang"), None)
    return jax.shard_map(
        per_device, mesh=mesh, in_specs=in_specs, out_specs=out_specs, check_vma=False
    )
```

time: 488 us -> 58 us (0.12)
  loops' own time: 185 us -> 0 us
  local copies, waits for them, and re-layouts: 177 us -> 3.73 us
  waiting for transfers between devices: 54.4 us -> 14.6 us
  other arithmetic: 37.8 us -> 1.61 us
  Pallas kernels: 0 us -> 28.6 us
  starting transfers between devices: 18.2 us -> 7.44 us
  matrix products: 11.1 us -> 1.2 us
    another operation x4 -> x0, loops' own time: 185 us -> none  [the longest x1 138 us: per_device(): lax.fori_loop(0, angles_here, blend_angle, (zeros_rows, zeros_rows))]
    dynamic_update_slice x160 -> x0, local copies, waits for them, and re-layouts: 130 us -> none  [the longest x72 54.8 us: blend_angle(): lax.dynamic_update_slice(weight_sum, current_w + weights[None, :], place)]
    all_to_all x4 -> x1, waiting for transfers between devices: 54.4 us -> 14.6 us  [per_device(): lax.all_to_all(outgoing.reshape(devices, capacity, tile_width + LANES), '...]
    dynamic_slice x58 -> x0, local copies, waits for them, and re-layouts: 35 us -> none  [the longest x8 5.57 us: blend_angle(): lax.dynamic_index_in_dim(section_offset, angle, 0, keepdims=False)]
    pallas_call x0 -> x1, Pallas kernels: none -> 28.6 us  [per_device(): pl.pallas_call(functools.partial(kernel, cfg), out_shape=jax.ShapeDtypeSt...]
    add x97 -> x0, other arithmetic: 11.7 us -> none  [the longest x72 8.21 us: blend_angle(): current_w + weights[None, :]]
    all_to_all x4 -> x1, starting transfers between devices: 18.2 us -> 7.44 us  [per_device(): lax.all_to_all(outgoing.reshape(devices, capacity, tile_width + LANES), '...]
    lt x16 -> x0, other arithmetic: 10.4 us -> none  [the longest x8 5.2 us: center_module(): valid = (window < module_width[module])[None, :]]
  transfers between devices with their start and end apart: 4 -> 1, of which waited for: 4 -> 1; matrix products, arithmetic and copies ran while one was open for 1% -> 1% of each run, Pallas kernels for 0% -> 0%
where the time goes in v1:
time: 58 us; the launch traced here: 57.2 us
  Pallas kernels  28.6 us (49%)
  waiting for transfers between devices  14.6 us (25%)
  starting transfers between devices  7.44 us (13%)
  local copies, waits for them, and re-layouts  3.73 us (6%)
  other arithmetic  1.61 us (3%)
  matrix products  1.2 us (2%)
    pallas_call x1, Pallas kernels, per_device(): pl.pallas_call(functools.partial(kernel, cfg), out_shape=jax.ShapeDtypeSt...  28.6 us
    all_to_all x1, waiting for transfers between devices, per_device(): lax.all_to_all(outgoing.reshape(devices, capacity, tile_width + LANES), '...  14.6 us
    all_to_all x1, starting transfers between devices, per_device(): lax.all_to_all(outgoing.reshape(devices, capacity, tile_width + LANES), '...  7.44 us
    unnamed x3, local copies, waits for them, and re-layouts  1.87 us
    dot_general x1, matrix products, per_device(): jnp.dot(send_match.astype(raw.dtype), extended, preferred_element_type=jn...  1.2 us
  transfers between devices with their start and end apart: 1, of which 1 were waited for; matrix products, arithmetic and copies ran while one was open for 1% of the time, Pallas kernels for 0%

profile of v1, /device:TPU:0, one launch (start us, length us, event | category | flops | bytes accessed | tf_op | source)
XLA Modules:
  0.0 57.2 jit_solution(16665697485096884240)
XLA Ops:
  0.0 0.7 %add_convert_fusion = (bf16[72]{0:T(256)(128)(2,1)S(1)}, s32[72]{0:T(128)S(1)}) fusion(s32[72]{0:T(128)} %param.9), kind=kLoop, calls=%fused_computation.11 | loop fusion | flops 864 | bytes 720 | tf_op jit(solution)/shard_map/convert_element_type | solution.py:356
  0.7 0.1 fusion.3
  0.8 0.1 reduce_window_sum.11
  0.9 0.2 select_reduce_fusion
  1.0 0.1 broadcast_in_dim.6
  1.1 1.2 %convolution_convert_fusion = bf16[72,2176]{1,0:T(8,128)(2,1)S(1)} fusion(bf16[72,128]{1,0:T(8,128)(2,1)S(1)} %broadcast_in_dim.6, bf16[72,2048]{1,0:T(8,128)(2,1)} %param.8, s32[72]{0:T(128)S(1)} %multiply_add_fusion), kind=kOutput, calls=%fused_computation | convolution fusion | flops 23349312 | bytes 626976 | tf_op jit(solution)/shard_map/dot_general | solution.py:360
  2.3 0.9 %reshape.9 = bf16[8,9,2176]{2,1,0:T(8,128)(2,1)} reshape(bf16[72,2176]{1,0:T(8,128)(2,1)S(1)} %convolution_convert_fusion) | data formatting | bytes 626688 | tf_op jit(solution)/shard_map/reshape | solution.py:364
  3.3 0.0 copy-start
  3.3 7.4 %all-to-all-start = ((bf16[8,9,2176]{2,1,0:T(8,128)(2,1)}), bf16[8,9,2176]{2,1,0:T(8,128)(2,1)S(1)}, u32[]{:S(2)}, u32[]{:S(2)}) async-start(bf16[8,9,2176]{2,1,0:T(8,128)(2,1)} %reshape.9), calls=%async_computation | async-start | bytes 1114112 | tf_op jit(solution)/shard_map/all_to_all | solution.py:363
  10.7 0.0 copy-done
  10.7 0.6 %convert_bitcast_fusion.width_ref = f32[1,16]{1,0:T(1,128)} fusion(s32[8]{0:T(128)S(1)} %copy-done), kind=kLoop, calls=%fused_computation.10 | loop fusion | flops 16 | bytes 96 | tf_op jit(solution)/shard_map/broadcast_in_dim | solution.py:375
  11.3 14.6 %all-to-all-done = bf16[8,9,2176]{2,1,0:T(8,128)(2,1)S(1)} async-done(((bf16[8,9,2176]{2,1,0:T(8,128)(2,1)}), bf16[8,9,2176]{2,1,0:T(8,128)(2,1)S(1)}, u32[]{:S(2)}, u32[]{:S(2)}) %all-to-all-start) | async-done | bytes 313376 | tf_op jit(solution)/shard_map/all_to_all | solution.py:363
  25.9 0.9 %reshape.10.arrived_ref = bf16[72,2176]{1,0:T(8,128)(2,1)} reshape(bf16[8,9,2176]{2,1,0:T(8,128)(2,1)S(1)} %all-to-all-done) | data formatting | bytes 626688 | tf_op jit(solution)/shard_map/reshape | solution.py:369
  26.7 28.6 %shard_map.82 = f32[8,16384]{1,0:T(8,128)} custom-call(bf16[72,2176]{1,0:T(8,128)(2,1)} %reshape.10.arrived_ref, s32[8,9]{1,0:T(8,128)} %offset_ref.1, s32[1,9]{1,0:T(1,128)} %bitcast.3, f32[1,16]{1,0:T(1,128)} %convert_bitcast_fusion.width_ref, bf16[2,160,128]{2,1,0:T(8,128)(2,1)} %constant.26.clone.fwd_ref, bf16[64,240]{1,0:T(8,128)(2,1)} %constant.27.clone.inv_ref, ...), custom_call_target="tpu_custom_call" | custom-call | tf_op jit(solution)/shard_map/pallas_call | solution.py:380
  55.3 1.9 %copy.10 = f32[8,16384]{1,0:T(8,128)} copy(f32[8,16384]{1,0:T(8,128)} %shard_map.82) | data formatting | bytes 1048576
  (1 shorter events, 0.0 us)
Async XLA Ops:
  3.3 7.4 %copy-start = (s32[8]{0:T(128)S(1)}, s32[8]{0:T(128)}, u32[]{:S(2)}) copy-start(s32[8]{0:T(128)} %param.12) | copy-start | bytes 100
  3.3 22.6 %all-to-all-start = ((bf16[8,9,2176]{2,1,0:T(8,128)(2,1)}), bf16[8,9,2176]{2,1,0:T(8,128)(2,1)S(1)}, u32[]{:S(2)}, u32[]{:S(2)}) async-start(bf16[8,9,2176]{2,1,0:T(8,128)(2,1)} %reshape.9), calls=%async_computation | async-start | bytes 1114112 | tf_op jit(solution)/shard_map/all_to_all | solution.py:363

commit v2 on v1

--- a/solution.py
+++ b/solution.py
@@ -110,7 +110,8 @@
 
 def kernel(
     cfg,
-    arrived_ref,
+    raw_ref,
+    dest_ref,
     offset_ref,
     ramp_ref,
     width_ref,
@@ -118,6 +119,8 @@
     inv_ref,
     taps_ref,
     out_ref,
+    rows_send,
+    rows_recv,
     grid_ref,
     sum_ref,
     weight_ref,
@@ -129,6 +132,8 @@
     level_recv,
     stripe_send,
     stripe_recv,
+    base_send,
+    base_recv,
     send_sem,
     recv_sem,
 ):
@@ -167,13 +172,85 @@
             device_id_type=pl.DeviceIdType.MESH,
         )
 
+    def finish(phase, send_of, recv_of):
+        def body(step):
+            peer = peer_at(step + 1)
+            copy = remote(phase, send_of(peer), recv_of(peer), peer, peer)
+            copy.wait_recv()
+            copy.wait_send()
+
+        loop(devices - 1, body)
+
+    cap = -(-blocks // devices)
+    slab = 16
+    chunks = tile_width // LANES
+    extra = chunks - cap
+    slots = devices * slab
+    dest_row = dest_ref[...].astype(F32)
+    source_row = iota((blocks, blocks), 1)
+    source_col = iota((blocks, blocks), 0)
+
+    def turned(values):
+        return jnp.sum(jnp.where(source_row == source_col, values, 0.0), axis=1, keepdims=True)
+
+    owner_row = jnp.floor((dest_row + 0.5) * (1.0 / blocks))
+    owner_col = turned(owner_row)
+    earlier = (owner_col == owner_row) & (source_col < source_row)
+    rank_row = jnp.sum(jnp.where(earlier, 1.0, 0.0), axis=0, keepdims=True)
+    rank_col = turned(rank_row)
+    place_col = turned(dest_row - owner_row * blocks + 1.0)
+    slot = iota((slots, 1), 0).astype(F32)
+
+    def one_hot(left, right):
+        return jnp.where(left == right, 1.0, 0.0).astype(BF16)
+
+    direct = one_hot(slot, owner_row * slab + rank_row)
+    packed = dot(direct, raw_ref[:, : cap * LANES])
+    keeps = [
+        jnp.where(jnp.broadcast_to(rank_col, (blocks, LANES)) == j, 1.0, 0.0).astype(BF16)
+        for j in range(cap)
+    ]
+    for e in range(extra):
+        chunk = raw_ref[:, (cap + e) * LANES : (cap + e + 1) * LANES]
+        masked = jnp.concatenate([chunk * keep for keep in keeps], axis=1)
+        packed = packed + dot(one_hot(slot, owner_row * slab + (cap + e)), masked)
+    places = dot(direct, jnp.broadcast_to(place_col, (blocks, LANES)).astype(BF16))
+    rows_send[:, :, : cap * LANES] = packed.astype(BF16).reshape(devices, slab, cap * LANES)
+    rows_send[:, :, cap * LANES :] = places.astype(BF16).reshape(devices, slab, LANES)
+
+    pl.semaphore_wait(barrier, devices - 1)
+
+    def send_rows(step):
+        peer = peer_at(step + 1)
+        remote(0, rows_send.at[peer], rows_recv.at[me], me, peer).start()
+
+    loop(devices - 1, send_rows)
+    rows_recv[me] = rows_send[me]
+    finish(0, lambda p: rows_send.at[p], lambda p: rows_recv.at[p])
+
     pick = (iota((8, LANES), 1) == 0).astype(F32).astype(BF16)
-    ids = dot_nt(pick, arrived_ref[:, tile_width:])[0:1, :]
+    ids = dot_nt(pick, rows_recv[:, :, cap * LANES :].reshape(slots, LANES))
     row = iota((blocks, 1), 0).astype(F32)
     tile_of = jnp.floor((row + 0.5) * (1.0 / angles_here))
     wanted = (row - tile_of * angles_here) * tiles + tile_of + 1.0
-    match = jnp.where(wanted == ids, 1.0, 0.0).astype(BF16)
-    grid_ref[...] = dot(match, arrived_ref[:, :tile_width])
+    lead = rows_recv[:, :, : cap * LANES].reshape(slots, cap * LANES)
+    grid_ref[:, : cap * LANES] = dot(one_hot(wanted, ids[0:1]), lead)
+    if extra:
+        within = iota((8, slots), 1) & (slab - 1)
+        turns = [pltpu.roll(ids, n, 1) if n else ids for n in range(slab)]
+        wanted_at = jnp.concatenate(
+            [jnp.where(within[0:1] == cap + e, wanted, -1.0) for e in range(extra)], axis=0
+        )
+        rest = jnp.zeros((extra * blocks, LANES), F32)
+        for j in range(cap):
+            ids_j = jnp.zeros((8, slots), F32)
+            for e in range(extra):
+                ids_j = jnp.where(within == cap + e, turns[cap + e - j], ids_j)
+            part = rows_recv[:, :, j * LANES : (j + 1) * LANES].reshape(slots, LANES)
+            rest = rest + dot(one_hot(wanted_at, ids_j[0:1]), part)
+        for e in range(extra):
+            at = (cap + e) * LANES
+            grid_ref[:, at : at + LANES] = rest[e * blocks : (e + 1) * blocks]
 
     sum_ref[...] = jnp.zeros_like(sum_ref)
     weight_ref[...] = jnp.zeros_like(weight_ref)
@@ -229,8 +306,6 @@
 
     mean = thirds(gather_thirds(total) / safe_wide)
 
-    pl.semaphore_wait(barrier, devices - 1)
-
     def centered_slab(owner):
         at = pl.multiple_of(owner * cols, LANES)
         flat = proj_ref[:, pl.ds(at, cols)] - gather_thirds(dot(mean, member(at, cols)))
@@ -241,21 +316,12 @@
     def send_centered(step):
         peer = peer_at(step + 1)
         cent_send[peer] = centered_slab(peer)
-        remote(0, cent_send.at[peer], cent_recv.at[me], me, peer).start()
+        remote(1, cent_send.at[peer], cent_recv.at[me], me, peer).start()
 
     loop(devices - 1, send_centered)
     cent_recv[me] = centered_slab(me)
 
-    def finish(phase, send_of, recv_of):
-        def body(step):
-            peer = peer_at(step + 1)
-            copy = remote(phase, send_of(peer), recv_of(peer), peer, peer)
-            copy.wait_recv()
-            copy.wait_send()
-
-        loop(devices - 1, body)
-
-    finish(0, lambda p: cent_send.at[p], lambda p: cent_recv.at[p])
+    finish(1, lambda p: cent_send.at[p], lambda p: cent_recv.at[p])
 
     signal = cent_recv[...].reshape(devices * fold * angles_here, half).astype(BF16)
     k = iota((rows, 1), 0)
@@ -278,15 +344,16 @@
 
     def send_level(step):
         peer = peer_at(step + 1)
-        remote(1, level_send, level_recv.at[me], me, peer).start()
+        remote(2, level_send, level_recv.at[me], me, peer).start()
 
     loop(devices - 1, send_level)
     level_recv[me] = level_send[...]
-    finish(1, lambda p: level_send, lambda p: level_recv.at[p])
+    finish(2, lambda p: level_send, lambda p: level_recv.at[p])
     everything = jnp.sum(level_recv[...], axis=0)[:, 0:mods]
     level = SHRINK_SCALE * (everything / (angles * safe_wide) + EPSILON)
     level_parts = thirds(jnp.where(iota((8, mods), 0) == 0, level, 0.0))
 
+    residual = []
     for part in range(fold):
         spread = dot(level_parts, member(mine + part * half, half))
         level_col = spread[0:1] + spread[8:9] + spread[16:17]
@@ -298,17 +365,22 @@
         shrunk = jnp.concatenate([spectrum[:rows] * factor, spectrum[rows:] * factor], axis=0)
         high, low = halves(shrunk)
         stripe = dot(inv_ref[...], jnp.concatenate([high, low, high], axis=0))
-        stripe_send[:, :, part * half : (part + 1) * half] = stripe.reshape(
-            devices, angles_here, half
-        )
+        stripe = stripe.reshape(devices, angles_here, half)
+        base = jnp.mean(stripe, axis=1, keepdims=True)
+        base_send[:, :, part * half : (part + 1) * half] = base
+        residual.append(stripe - base)
+    stripe_send[...] = jnp.concatenate(residual, axis=1).astype(stripe_send.dtype)
 
     def send_stripe(step):
         peer = peer_at(step + 1)
-        remote(2, stripe_send.at[peer], stripe_recv.at[me], me, peer).start()
+        remote(3, stripe_send.at[peer], stripe_recv.at[me], me, peer).start()
+        remote(4, base_send.at[peer], base_recv.at[me], me, peer).start()
 
     loop(devices - 1, send_stripe)
     stripe_recv[me] = stripe_send[me]
-    finish(2, lambda p: stripe_send.at[p], lambda p: stripe_recv.at[p])
+    base_recv[me] = base_send[me]
+    finish(3, lambda p: stripe_send.at[p], lambda p: stripe_recv.at[p])
+    finish(4, lambda p: base_send.at[p], lambda p: base_recv.at[p])
 
     sum_ref[:, 0:LANES] = jnp.zeros((angles_here, LANES), F32)
     sum_ref[:, W + LANES :] = jnp.zeros((angles_here, LANES), F32)
@@ -316,7 +388,12 @@
     def clean(owner):
         at = pl.multiple_of(owner * cols, LANES)
         behind = pl.multiple_of(owner * cols + LANES, LANES)
-        sum_ref[:, pl.ds(behind, cols)] = proj_ref[:, pl.ds(at, cols)] - stripe_recv[owner]
+        rest = stripe_recv[owner].astype(F32)
+        rest = jnp.concatenate(
+            [rest[i * angles_here : (i + 1) * angles_here] for i in range(fold)], axis=1
+        )
+        stripe = rest + base_recv[owner]
+        sum_ref[:, pl.ds(behind, cols)] = proj_ref[:, pl.ds(at, cols)] - stripe
 
     loop(devices, clean)
     lane_blocks = SPAN // LANES
@@ -348,26 +425,6 @@
     angles_here, tiles = section_offset.shape
     angles = angles_here * devices
     capacity = (blocks_here + devices - 1) // devices
-    owners = block_dest // blocks_here
-    owner_hot = (owners[:, None] == jnp.arange(devices, dtype=jnp.int32)[None, :]).astype(jnp.int32)
-    slot_rank = jnp.sum((jnp.cumsum(owner_hot, axis=0) - owner_hot) * owner_hot, axis=1)
-    slot = owners * capacity + slot_rank
-    send_match = jnp.arange(devices * capacity, dtype=jnp.int32)[:, None] == slot[None, :]
-    local_id = (block_dest - owners * blocks_here + 1).astype(raw.dtype)
-    extended = jnp.concatenate(
-        [raw, jnp.broadcast_to(local_id[:, None], (blocks_here, LANES))], axis=1
-    )
-    outgoing = jnp.dot(
-        send_match.astype(raw.dtype), extended, preferred_element_type=jnp.float32
-    ).astype(raw.dtype)
-    arrived = lax.all_to_all(
-        outgoing.reshape(devices, capacity, tile_width + LANES),
-        "ang",
-        split_axis=0,
-        concat_axis=0,
-        tiled=True,
-    ).reshape(devices * capacity, tile_width + LANES)
-
     cols = W // devices
     fold = 2 if cols % (2 * LANES) == 0 else 1
     wire = BF16 if fold == 2 else F32
@@ -380,9 +437,11 @@
     return pl.pallas_call(
         functools.partial(kernel, cfg),
         out_shape=jax.ShapeDtypeStruct((angles_here, W), F32),
-        in_specs=[vmem] * 7,
+        in_specs=[vmem] * 8,
         out_specs=vmem,
         scratch_shapes=[
+            pltpu.VMEM((devices, 16, (capacity + 1) * LANES), BF16),
+            pltpu.VMEM((devices, 16, (capacity + 1) * LANES), BF16),
             pltpu.VMEM((angles_here * tiles, tile_width), F32),
             pltpu.VMEM((angles_here, W + 2 * LANES), F32),
             pltpu.VMEM((angles_here, W + 2 * LANES), F32),
@@ -392,16 +451,19 @@
             pltpu.VMEM((fold, 2 * rows, half), F32),
             pltpu.VMEM((8, max(mods, LANES)), F32),
             pltpu.VMEM((devices, 8, max(mods, LANES)), F32),
-            pltpu.VMEM((devices, angles_here, cols), F32),
-            pltpu.VMEM((devices, angles_here, cols), F32),
-            pltpu.SemaphoreType.DMA((3, devices)),
-            pltpu.SemaphoreType.DMA((3, devices)),
+            pltpu.VMEM((devices, angles_here * fold, half), wire),
+            pltpu.VMEM((devices, angles_here * fold, half), wire),
+            pltpu.VMEM((devices, 1, cols), F32),
+            pltpu.VMEM((devices, 1, cols), F32),
+            pltpu.SemaphoreType.DMA((5, devices)),
+            pltpu.SemaphoreType.DMA((5, devices)),
         ],
         compiler_params=pltpu.CompilerParams(
             collective_id=0, has_side_effects=True, vmem_limit_bytes=60 << 20
         ),
     )(
-        arrived,
+        raw,
+        block_dest[None, :],
         section_offset,
         ramp_length[None, :],
         widths,

time: 58 us -> 43.8 us (0.76)
  waiting for transfers between devices: 14.6 us -> 0 us
  Pallas kernels: 28.6 us -> 40.5 us
  starting transfers between devices: 7.44 us -> 0 us
  local copies, waits for them, and re-layouts: 3.73 us -> 2.52 us
  matrix products: 1.2 us -> 0 us
  other arithmetic: 1.61 us -> 0.51 us
    all_to_all x1 -> x0, waiting for transfers between devices: 14.6 us -> none  [per_device(): lax.all_to_all(outgoing.reshape(devices, capacity, tile_width + LANES), '...]
    pallas_call x1, Pallas kernels: 28.6 us -> 40.5 us  [per_device(): pl.pallas_call(functools.partial(kernel, cfg), out_shape=jax.ShapeDtypeSt...]
    all_to_all x1 -> x0, starting transfers between devices: 7.44 us -> none  [per_device(): lax.all_to_all(outgoing.reshape(devices, capacity, tile_width + LANES), '...]
    reshape x2 -> x0, local copies, waits for them, and re-layouts: 1.78 us -> none  [the longest x1 0.92 us: per_device(): outgoing.reshape(devices, capacity, tile_width + LANES)]
    dot_general x1 -> x0, matrix products: 1.2 us -> none  [per_device(): jnp.dot(send_match.astype(raw.dtype), extended, preferred_element_type=jn...]
    convert_element_type x2 -> x0, other arithmetic: 0.74 us -> none  [the longest x1 0.67 us: per_device(): local_id = (block_dest - owners * blocks_here + 1).astype(raw.dtype)]
    unnamed x3, local copies, waits for them, and re-layouts: 1.87 us -> 2.52 us
  transfers between devices with their start and end apart: 1 -> 0, of which waited for: 1 -> 0; matrix products, arithmetic and copies ran while one was open for 1% -> 0% of each run, Pallas kernels for 0% -> 0%
where the time goes in v2:
time: 43.8 us; the launch traced here: 43.6 us
  Pallas kernels  40.5 us (92%)
  local copies, waits for them, and re-layouts  2.52 us (6%)
  other arithmetic  0.51 us (1%)
    pallas_call x1, Pallas kernels, per_device(): pl.pallas_call(functools.partial(kernel, cfg), out_shape=jax.ShapeDtypeSt...  40.5 us
    unnamed x3, local copies, waits for them, and re-layouts  2.52 us

profile of v2, /device:TPU:0, one launch (start us, length us, event | category | flops | bytes accessed | tf_op | source)
XLA Modules:
  0.0 43.6 jit_solution(13359964490973749280)
XLA Ops:
  0.0 0.0 copy-start
  0.0 0.7 %copy-done = s32[8]{0:T(128)S(1)} copy-done((s32[8]{0:T(128)S(1)}, s32[8]{0:T(128)}, u32[]{:S(2)}) %copy-start) | copy-done | bytes 56
  0.7 0.5 %convert_bitcast_fusion.width_ref = f32[1,16]{1,0:T(1,128)} fusion(s32[8]{0:T(128)S(1)} %copy-done), kind=kLoop, calls=%fused_computation | loop fusion | flops 16 | bytes 96 | tf_op jit(solution)/shard_map/broadcast_in_dim | solution.py:432
  1.2 40.5 %shard_map.82 = f32[8,16384]{1,0:T(8,128)} custom-call(bf16[72,2048]{1,0:T(8,128)(2,1)} %raw_ref.1, s32[1,72]{1,0:T(1,128)} %bitcast.4, s32[8,9]{1,0:T(8,128)} %offset_ref.1, s32[1,9]{1,0:T(1,128)} %bitcast.5, f32[1,16]{1,0:T(1,128)} %convert_bitcast_fusion.width_ref, bf16[2,160,128]{2,1,0:T(8,128)(2,1)} %constant.8.clone.fwd_ref, ...), custom_call_target="tpu_custom_call" | custom-call | tf_op jit(solution)/shard_map/pallas_call | solution.py:437
  41.7 1.9 %copy.10 = f32[8,16384]{1,0:T(8,128)} copy(f32[8,16384]{1,0:T(8,128)} %shard_map.82) | data formatting | bytes 1048576
Async XLA Ops:
  0.0 0.7 %copy-start = (s32[8]{0:T(128)S(1)}, s32[8]{0:T(128)}, u32[]{:S(2)}) copy-start(s32[8]{0:T(128)} %param.12) | copy-start | bytes 100

commit v3 on v2

--- a/solution.py
+++ b/solution.py
@@ -115,9 +115,9 @@
     offset_ref,
     ramp_ref,
     width_ref,
-    fwd_ref,
-    inv_ref,
-    taps_ref,
+    fwd_hbm,
+    inv_hbm,
+    taps_hbm,
     out_ref,
     rows_send,
     rows_recv,
@@ -134,6 +134,10 @@
     stripe_recv,
     base_send,
     base_recv,
+    fwd_ref,
+    inv_ref,
+    taps_ref,
+    table_sem,
     send_sem,
     recv_sem,
 ):
@@ -161,6 +165,12 @@
         )
 
     loop(devices - 1, greet)
+    fetch_fwd = pltpu.make_async_copy(fwd_hbm, fwd_ref, table_sem.at[0])
+    fetch_inv = pltpu.make_async_copy(inv_hbm, inv_ref, table_sem.at[1])
+    fetch_taps = pltpu.make_async_copy(taps_hbm, taps_ref, table_sem.at[2])
+    fetch_fwd.start()
+    fetch_inv.start()
+    fetch_taps.start()
 
     def remote(phase, src, dst, slot, peer):
         return pltpu.make_async_remote_copy(
@@ -252,6 +262,10 @@
             at = (cap + e) * LANES
             grid_ref[:, at : at + LANES] = rest[e * blocks : (e + 1) * blocks]
 
+    fetch_fwd.wait()
+    fetch_inv.wait()
+    fetch_taps.wait()
+
     sum_ref[...] = jnp.zeros_like(sum_ref)
     weight_ref[...] = jnp.zeros_like(weight_ref)
     inverse_ramp = 1.0 / ramp_ref[...].astype(F32)
@@ -278,12 +292,14 @@
         sum_ref[:, base : base + window] += feather * piece
         weight_ref[:, base : base + window] += feather
 
-    wide = width_ref[...]
-    upper = iota((mods, mods), 1)
-    lower = iota((mods, mods), 0)
+    wide = width_ref[...].astype(F32)
+    upper = iota((mods, wide.shape[1]), 1)
+    lower = iota((mods, wide.shape[1]), 0)
     bounds = jnp.sum(jnp.where(upper <= lower, wide, 0.0), axis=1, keepdims=True)
     starts = jnp.sum(jnp.where(upper < lower, wide, 0.0), axis=1, keepdims=True)
-    safe_wide = jnp.maximum(wide, 1.0)
+    on_diagonal = iota((mods, mods), 0) == iota((mods, mods), 1)
+    safe_wide = jnp.sum(jnp.where(on_diagonal, bounds - starts, 0.0), axis=0, keepdims=True)
+    safe_wide = jnp.maximum(safe_wide, 1.0)
 
     def member(first, count):
         c = (iota((mods, count), 1) + first).astype(F32)
@@ -291,14 +307,16 @@
         return jnp.where(inside, 1.0, 0.0).astype(BF16)
 
     def project(step, total):
-        at = pl.multiple_of(step * SPAN, LANES)
-        behind = pl.multiple_of(step * SPAN + LANES, LANES)
+        at = step * SPAN
+        behind = at + LANES
         blended = sum_ref[:, pl.ds(behind, SPAN)] / weight_ref[:, pl.ds(behind, SPAN)]
         projection = -jnp.log(blended)
         proj_ref[:, pl.ds(at, SPAN)] = projection
         return total + dot_nt(thirds(projection), member(at, SPAN))
 
-    total = lax.fori_loop(0, W // SPAN, project, jnp.zeros((4 * angles_here, mods), F32))
+    total = jnp.zeros((4 * angles_here, mods), F32)
+    for step in range(W // SPAN):
+        total = project(step, total)
 
     def gather_thirds(stack):
         a = angles_here
@@ -379,11 +397,10 @@
     loop(devices - 1, send_stripe)
     stripe_recv[me] = stripe_send[me]
     base_recv[me] = base_send[me]
-    finish(3, lambda p: stripe_send.at[p], lambda p: stripe_recv.at[p])
-    finish(4, lambda p: base_send.at[p], lambda p: base_recv.at[p])
 
     sum_ref[:, 0:LANES] = jnp.zeros((angles_here, LANES), F32)
     sum_ref[:, W + LANES :] = jnp.zeros((angles_here, LANES), F32)
+    lane_blocks = cols // LANES
 
     def clean(owner):
         at = pl.multiple_of(owner * cols, LANES)
@@ -395,12 +412,9 @@
         stripe = rest + base_recv[owner]
         sum_ref[:, pl.ds(behind, cols)] = proj_ref[:, pl.ds(at, cols)] - stripe
 
-    loop(devices, clean)
-    lane_blocks = SPAN // LANES
-
-    def ramp(step, carry):
-        at = pl.multiple_of(step * SPAN, LANES)
-        flat = sum_ref[:, pl.ds(at, SPAN + 2 * LANES)]
+    def ramp(group):
+        at = pl.multiple_of(group * cols, LANES)
+        flat = sum_ref[:, pl.ds(at, cols + 2 * LANES)]
         stack = jnp.concatenate(
             [flat[:, b * LANES : (b + 1) * LANES] for b in range(lane_blocks + 2)], axis=0
         )
@@ -410,12 +424,37 @@
         )
         high, low = halves(near)
         done = dot(high, taps_ref[0]) + dot(low, taps_ref[0]) + dot(high, taps_ref[1])
-        out_ref[:, pl.ds(at, SPAN)] = jnp.concatenate(
+        out_ref[:, pl.ds(at, cols)] = jnp.concatenate(
             [done[b * angles_here : (b + 1) * angles_here] for b in range(lane_blocks)], axis=1
         )
-        return carry
-
-    lax.fori_loop(0, W // SPAN, ramp, 0)
+
+    clean(me)
+
+    def below(hop):
+        return lax.rem(me + devices - hop, devices)
+
+    def take(hop):
+        owner = below(hop)
+        remote(3, stripe_send.at[owner], stripe_recv.at[owner], owner, owner).wait_recv()
+        remote(4, base_send.at[owner], base_recv.at[owner], owner, owner).wait_recv()
+        clean(owner)
+
+    take(1)
+
+    def advance(step):
+        take(step + 2)
+        ramp(below(step + 1))
+
+    loop(devices - 2, advance)
+    ramp(below(devices - 1))
+    ramp(me)
+
+    def sent(step):
+        peer = peer_at(step + 1)
+        remote(3, stripe_send.at[peer], stripe_recv.at[peer], peer, peer).wait_send()
+        remote(4, base_send.at[peer], base_recv.at[peer], peer, peer).wait_send()
+
+    loop(devices - 1, sent)
 
 
 def per_device(raw, block_dest, section_offset, ramp_length, module_width):
@@ -429,15 +468,17 @@
     fold = 2 if cols % (2 * LANES) == 0 else 1
     wire = BF16 if fold == 2 else F32
     mods = -(-module_width.shape[0] // 16) * 16
-    widths = jnp.pad(module_width, (0, mods - module_width.shape[0])).astype(F32)[None, :]
     half = cols // fold
     rows = freq_rows(angles)
     cfg = (devices, angles_here, tiles, tile_width, mods, fold)
+    forward = forward_table(angles, devices, fold)
+    inverse = inverse_table(angles)
+    taps = ramp_table()
     vmem = pl.BlockSpec(memory_space=pltpu.VMEM)
     return pl.pallas_call(
         functools.partial(kernel, cfg),
         out_shape=jax.ShapeDtypeStruct((angles_here, W), F32),
-        in_specs=[vmem] * 8,
+        in_specs=[vmem] * 5 + [pl.BlockSpec(memory_space=pl.ANY)] * 3,
         out_specs=vmem,
         scratch_shapes=[
             pltpu.VMEM((devices, 16, (capacity + 1) * LANES), BF16),
@@ -455,6 +496,10 @@
             pltpu.VMEM((devices, angles_here * fold, half), wire),
             pltpu.VMEM((devices, 1, cols), F32),
             pltpu.VMEM((devices, 1, cols), F32),
+            pltpu.VMEM(forward.shape, BF16),
+            pltpu.VMEM(inverse.shape, BF16),
+            pltpu.VMEM(taps.shape, BF16),
+            pltpu.SemaphoreType.DMA((3,)),
             pltpu.SemaphoreType.DMA((5, devices)),
             pltpu.SemaphoreType.DMA((5, devices)),
         ],
@@ -466,10 +511,10 @@
         block_dest[None, :],
         section_offset,
         ramp_length[None, :],
-        widths,
-        jnp.asarray(forward_table(angles, devices, fold)),
-        jnp.asarray(inverse_table(angles)),
-        jnp.asarray(ramp_table()),
+        module_width[None, :],
+        jnp.asarray(forward),
+        jnp.asarray(inverse),
+        jnp.asarray(taps),
     )
 
 

time: 43.8 us -> 41.5 us (0.947)
  Pallas kernels: 40.5 us -> 39.4 us
  local copies, waits for them, and re-layouts: 2.52 us -> 1.87 us
  other arithmetic: 0.51 us -> 0 us
    pallas_call x1, Pallas kernels: 40.5 us -> 39.4 us  [per_device(): pl.pallas_call(functools.partial(kernel, cfg), out_shape=jax.ShapeDtypeSt...]
    unnamed x3 -> x1, local copies, waits for them, and re-layouts: 2.52 us -> 1.87 us
    broadcast_in_dim x1 -> x0, other arithmetic: 0.51 us -> none  [per_device(): jnp.pad(module_width, (0, mods - module_width.shape[0])).astype(F32)]
where the time goes in v3:
time: 41.5 us; the launch traced here: 41.3 us
  Pallas kernels  39.4 us (95%)
  local copies, waits for them, and re-layouts  1.87 us (5%)
    pallas_call x1, Pallas kernels, per_device(): pl.pallas_call(functools.partial(kernel, cfg), out_shape=jax.ShapeDtypeSt...  39.4 us
    unnamed x1, local copies, waits for them, and re-layouts  1.87 us

profile of v3, /device:TPU:0, one launch (start us, length us, event | category | flops | bytes accessed | tf_op | source)
XLA Modules:
  0.0 41.3 jit_solution(5484142917010091690)
XLA Ops:
  0.0 39.4 %shard_map.82 = f32[8,16384]{1,0:T(8,128)} custom-call(bf16[72,2048]{1,0:T(8,128)(2,1)} %raw_ref.1, s32[1,72]{1,0:T(1,128)} %bitcast.3, s32[8,9]{1,0:T(8,128)} %offset_ref.1, s32[1,9]{1,0:T(1,128)} %bitcast.4, s32[1,8]{1,0:T(1,128)} %bitcast.5, bf16[2,160,128]{2,1,0:T(8,128)(2,1)} %constant.6.clone.fwd_hbm, bf16[64,240]{1,0:T(8,128)(2,1)} %constant.7.clone.inv_hbm, ...), custom_call_target="tpu_custom_call" | custom-call | tf_op jit(solution)/shard_map/pallas_call | solution.py:478
  39.4 1.9 %copy.10 = f32[8,16384]{1,0:T(8,128)} copy(f32[8,16384]{1,0:T(8,128)} %shard_map.82) | data formatting | bytes 1048576

commit v4 on v3

--- a/solution.py
+++ b/solution.py
@@ -151,8 +151,19 @@
     blocks = angles_here * tiles
     me = lax.axis_index("ang")
 
+    def ring_at(hop):
+        return lax.rem(me + hop, devices)
+
     def peer_at(hop):
-        return lax.rem(me + hop, devices)
+        if devices & (devices - 1):
+            return ring_at(hop)
+        mask = devices - hop
+        peer = 0
+        bit = 1
+        while bit < devices:
+            peer = peer + bit * lax.rem(lax.div(me, bit) + mask // bit, 2)
+            bit *= 2
+        return peer
 
     barrier = pltpu.get_barrier_semaphore()
 
@@ -390,7 +401,7 @@
     stripe_send[...] = jnp.concatenate(residual, axis=1).astype(stripe_send.dtype)
 
     def send_stripe(step):
-        peer = peer_at(step + 1)
+        peer = ring_at(step + 1)
         remote(3, stripe_send.at[peer], stripe_recv.at[me], me, peer).start()
         remote(4, base_send.at[peer], base_recv.at[me], me, peer).start()
 
@@ -450,11 +461,15 @@
     ramp(me)
 
     def sent(step):
-        peer = peer_at(step + 1)
+        peer = ring_at(step + 1)
         remote(3, stripe_send.at[peer], stripe_recv.at[peer], peer, peer).wait_send()
         remote(4, base_send.at[peer], base_recv.at[peer], peer, peer).wait_send()
 
     loop(devices - 1, sent)
+
+
+def put_out(in_ref, out_ref):
+    out_ref[...] = in_ref[...]
 
 
 def per_device(raw, block_dest, section_offset, ramp_length, module_width):
@@ -475,7 +490,7 @@
     inverse = inverse_table(angles)
     taps = ramp_table()
     vmem = pl.BlockSpec(memory_space=pltpu.VMEM)
-    return pl.pallas_call(
+    filtered = pl.pallas_call(
         functools.partial(kernel, cfg),
         out_shape=jax.ShapeDtypeStruct((angles_here, W), F32),
         in_specs=[vmem] * 5 + [pl.BlockSpec(memory_space=pl.ANY)] * 3,
@@ -517,6 +532,15 @@
         jnp.asarray(taps),
     )
 
+    block = pl.BlockSpec((angles_here, 2 * SPAN), lambda step: (0, step))
+    return pl.pallas_call(
+        put_out,
+        grid=(W // (2 * SPAN),),
+        out_shape=jax.ShapeDtypeStruct((angles_here, W), F32),
+        in_specs=[block],
+        out_specs=block,
+    )(filtered)
+
 
 def solution(mesh):
     in_specs = (P(("row", "ang"), None), P("ang"), P("ang", None), P(), P())

time: 41.5 us -> 40.6 us (0.978)
  local copies, waits for them, and re-layouts: 1.87 us -> 0 us
  Pallas kernels: 39.4 us -> 40.4 us
    pallas_call x0 -> x1, Pallas kernels: none -> 3.16 us  [per_device(): pl.pallas_call(put_out, grid=(W // (2 * SPAN),), out_shape=jax.ShapeDtype...]
    pallas_call x1, Pallas kernels: 39.4 us -> 37.2 us  [per_device(): pl.pallas_call(functools.partial(kernel, cfg), out_shape=jax.ShapeDtypeSt...]
    unnamed x1 -> x0, local copies, waits for them, and re-layouts: 1.87 us -> none
where the time goes in v4:
time: 40.6 us; the launch traced here: 40.4 us
  Pallas kernels  40.4 us (100%)
    pallas_call x1, Pallas kernels, per_device(): pl.pallas_call(functools.partial(kernel, cfg), out_shape=jax.ShapeDtypeSt...  37.2 us
    pallas_call x1, Pallas kernels, per_device(): pl.pallas_call(put_out, grid=(W // (2 * SPAN),), out_shape=jax.ShapeDtype...  3.16 us

profile of v4, /device:TPU:0, one launch (start us, length us, event | category | flops | bytes accessed | tf_op | source)
XLA Modules:
  0.0 40.4 jit_solution(16158143727325174)
XLA Ops:
  0.0 37.2 %shard_map.82.in_ref = f32[8,16384]{1,0:T(8,128)} custom-call(bf16[72,2048]{1,0:T(8,128)(2,1)} %raw_ref.1, s32[1,72]{1,0:T(1,128)} %bitcast.3, s32[8,9]{1,0:T(8,128)} %offset_ref.1, s32[1,9]{1,0:T(1,128)} %bitcast.4, s32[1,8]{1,0:T(1,128)} %bitcast.5, bf16[2,160,128]{2,1,0:T(8,128)(2,1)} %constant.6.clone.fwd_hbm, bf16[64,240]{1,0:T(8,128)(2,1)} %constant.7.clone.inv_hbm, ...), custom_call_target="tpu_custom_call" | custom-call | tf_op jit(solution)/shard_map/pallas_call | solution.py:493
  37.2 3.2 %shard_map.83 = f32[8,16384]{1,0:T(8,128)} custom-call(f32[8,16384]{1,0:T(8,128)} %shard_map.82.in_ref), custom_call_target="tpu_custom_call" | custom-call | tf_op jit(solution)/shard_map/pallas_call | solution.py:536

commit v5 on v4

--- a/solution.py
+++ b/solution.py
@@ -468,10 +468,6 @@
     loop(devices - 1, sent)
 
 
-def put_out(in_ref, out_ref):
-    out_ref[...] = in_ref[...]
-
-
 def per_device(raw, block_dest, section_offset, ramp_length, module_width):
     devices = lax.axis_size("ang")
     blocks_here = raw.shape[0]
@@ -490,7 +486,7 @@
     inverse = inverse_table(angles)
     taps = ramp_table()
     vmem = pl.BlockSpec(memory_space=pltpu.VMEM)
-    filtered = pl.pallas_call(
+    return pl.pallas_call(
         functools.partial(kernel, cfg),
         out_shape=jax.ShapeDtypeStruct((angles_here, W), F32),
         in_specs=[vmem] * 5 + [pl.BlockSpec(memory_space=pl.ANY)] * 3,
@@ -532,15 +528,6 @@
         jnp.asarray(taps),
     )
 
-    block = pl.BlockSpec((angles_here, 2 * SPAN), lambda step: (0, step))
-    return pl.pallas_call(
-        put_out,
-        grid=(W // (2 * SPAN),),
-        out_shape=jax.ShapeDtypeStruct((angles_here, W), F32),
-        in_specs=[block],
-        out_specs=block,
-    )(filtered)
-
 
 def solution(mesh):
     in_specs = (P(("row", "ang"), None), P("ang"), P("ang", None), P(), P())

time: 40.6 us -> 39.3 us (0.968)
  Pallas kernels: 40.4 us -> 37.2 us
  local copies, waits for them, and re-layouts: 0 us -> 1.87 us
    pallas_call x1 -> x0, Pallas kernels: 3.16 us -> none  [per_device(): pl.pallas_call(put_out, grid=(W // (2 * SPAN),), out_shape=jax.ShapeDtype...]
    unnamed x0 -> x1, local copies, waits for them, and re-layouts: none -> 1.87 us
where the time goes in v5:
time: 39.3 us; the launch traced here: 39.1 us
  Pallas kernels  37.2 us (95%)
  local copies, waits for them, and re-layouts  1.87 us (5%)
    pallas_call x1, Pallas kernels, per_device(): pl.pallas_call(functools.partial(kernel, cfg), out_shape=jax.ShapeDtypeSt...  37.2 us
    unnamed x1, local copies, waits for them, and re-layouts  1.87 us

profile of v5, /device:TPU:0, one launch (start us, length us, event | category | flops | bytes accessed | tf_op | source)
XLA Modules:
  0.0 39.1 jit_solution(14183199167421371169)
XLA Ops:
  0.0 37.2 %shard_map.82 = f32[8,16384]{1,0:T(8,128)} custom-call(bf16[72,2048]{1,0:T(8,128)(2,1)} %raw_ref.1, s32[1,72]{1,0:T(1,128)} %bitcast.3, s32[8,9]{1,0:T(8,128)} %offset_ref.1, s32[1,9]{1,0:T(1,128)} %bitcast.4, s32[1,8]{1,0:T(1,128)} %bitcast.5, bf16[2,160,128]{2,1,0:T(8,128)(2,1)} %constant.6.clone.fwd_hbm, bf16[64,240]{1,0:T(8,128)(2,1)} %constant.7.clone.inv_hbm, ...), custom_call_target="tpu_custom_call" | custom-call | tf_op jit(solution)/shard_map/pallas_call | solution.py:489
  37.2 1.9 %copy.10 = f32[8,16384]{1,0:T(8,128)} copy(f32[8,16384]{1,0:T(8,128)} %shard_map.82) | data formatting | bytes 1048576
